TPU v7x, 128 devices: a whole 4x4x4 slice. The times are simulated.
128 devices in a mesh: row: 8 (over x, z_hi), col: 16 (over z_lo, y, core).
Axes of the slice: x: 4, y: 4, z: 4 (z_hi: 2, z_lo: 2; z = z_hi * 2 + z_lo), core: 2. Of those that a mesh axis runs over, the one named last changes fastest.
Arguments:
- pair_state: bfloat16 [768, 768, 128], P(('row', 'col')), may hold values from -6 to 6
- single_rep: bfloat16 [16, 768, 768], P(None, ('row', 'col')), may hold values from -64 to 64
- token_mask: int32 [768], replicated, may hold values 0 or 1
- chain_ids: int32 [768], replicated, may hold values from 0 to 3, never falling along the last dimension, each value on 1 to 384 neighbouring positions
- pair_gain: float32 [128], replicated, may hold values from 0.1 to 1.9
- mix_gain: float32 [128], replicated, may hold values from 0.1 to 1.9
- left_weight: bfloat16 [128, 256], replicated, may hold values from -0.5 to 0.5
- right_weight: bfloat16 [128, 256], replicated, may hold values from -0.5 to 0.5
- gate_weight: bfloat16 [128, 128], replicated, may hold values from -0.5 to 0.5
- out_weight: bfloat16 [128, 128], replicated, may hold values from -0.5 to 0.5
- bias_weight: bfloat16 [128, 16], replicated, may hold values from -1.5 to 1.5
- token_weight: bfloat16 [768, 2304], replicated, may hold values from -0.21875 to 0.21875
- merge_weight: bfloat16 [768, 768], replicated, may hold values from -0.625 to 0.625
Outputs:
- pair_tiles: bfloat16 [768, 8, 16, 6, 128], P('row', None, 'col')
- attention_out: bfloat16 [16, 768, 768], P(None, ('row', 'col'))
Inputs may be any that keep to these rules, and one draw needn't show every extreme that they name: chain_ids never falls along the tokens; a chain holds 1 to 384 tokens.
All inputs are finite; a program needn't handle non-finite values.
Results may differ from a plain program's by a relative error of at most 0.034.
Values may be sent and summed in bfloat16 or wider, within the bound.
A program may use at most 256 MiB of HBM per device.

v0:
```python
import math
import jax
import jax.numpy as jnp
from jax import lax
from jax.sharding import PartitionSpec as P

epsilon = 1e-05


def normalize(values, norm_gain):
    floats = values.astype(jnp.float32)
    centered = floats - jnp.mean(floats, axis=-1, keepdims=True)
    variance = jnp.mean(centered * centered, axis=-1, keepdims=True)
    scaled = centered * lax.rsqrt(variance + epsilon)
    if norm_gain is None:
        return scaled
    return scaled * norm_gain


def gated_branch(normed, weight, pair_mask):
    half_width = weight.shape[0]
    hidden = jnp.einsum("ikc,ce->ike", normed, weight, preferred_element_type=jnp.float32)
    return (
        jax.nn.sigmoid(hidden[..., :half_width]) * hidden[..., half_width:] * pair_mask[..., None]
    ).astype(jnp.bfloat16)


def rows_blocks(pair_rows, valid_rows, valid_all, pair_gain, left_weight, group_count, group_rows):
    token_count = pair_rows.shape[1]
    channels = pair_rows.shape[2]

    def one_group(inputs):
        pair_group, valid_group = inputs
        normed_group = normalize(pair_group, pair_gain).astype(jnp.bfloat16)
        left_group = gated_branch(
            normed_group, left_weight, valid_group[:, None] * valid_all[None, :]
        )
        return (normed_group, left_group)

    grouped = (
        pair_rows.reshape(group_count, group_rows, token_count, channels),
        valid_rows.reshape(group_count, group_rows),
    )
    normed_groups, left_groups = lax.map(one_group, grouped)
    return (
        normed_groups.reshape(group_count * group_rows, token_count, channels),
        left_groups.reshape(group_count * group_rows, token_count, channels),
    )


def shards(
    pair_state,
    single_rep,
    token_mask,
    chain_ids,
    pair_gain,
    mix_gain,
    left_weight,
    right_weight,
    gate_weight,
    out_weight,
    bias_weight,
    token_weight,
    merge_weight,
):
    row_count = lax.axis_size("row")
    col_count = lax.axis_size("col")
    row_index = lax.axis_index("row")
    col_index = lax.axis_index("col")
    flat_rows = pair_state.shape[0]
    channels = pair_state.shape[2]
    samples = single_rep.shape[0]
    model_width = single_rep.shape[2]
    head_count = bias_weight.shape[1]
    head_width = model_width // head_count
    block_rows = flat_rows * col_count
    block_cols = flat_rows * row_count
    valid_all = (token_mask == 1).astype(jnp.float32)
    own_start = (row_index * col_count + col_index) * flat_rows
    row_start = row_index * block_rows
    valid_own = lax.dynamic_slice_in_dim(valid_all, own_start, flat_rows)
    valid_rows = lax.dynamic_slice_in_dim(valid_all, row_start, block_rows)
    valid_cols = lax.dynamic_index_in_dim(
        valid_all.reshape(row_count, col_count, flat_rows), col_index, 1, False
    ).reshape(block_cols)
    chain_rows = lax.dynamic_slice_in_dim(chain_ids, row_start, block_rows)
    chain_cols = lax.dynamic_index_in_dim(
        chain_ids.reshape(row_count, col_count, flat_rows), col_index, 1, False
    ).reshape(block_cols)
    projected = jnp.einsum(
        "std,de->ste", single_rep, token_weight, preferred_element_type=jnp.float32
    ).astype(jnp.bfloat16)
    queries = projected[..., :model_width]
    keys_own = projected[..., model_width : 2 * model_width]
    values_own = projected[..., 2 * model_width :]
    normed_own = normalize(pair_state, pair_gain).astype(jnp.bfloat16)
    own_mask = valid_own[:, None] * valid_all[None, :]
    right_own = gated_branch(normed_own, right_weight, own_mask)
    right_cols, keys_cols, values_cols = (
        lax.all_gather(right_own, "row", axis=0, tiled=True),
        lax.all_gather(keys_own, "row", axis=1, tiled=True),
        lax.all_gather(values_own, "row", axis=1, tiled=True),
    )
    pair_rows, query_rows = (
        lax.all_gather(pair_state, "col", axis=0, tiled=True),
        lax.all_gather(queries, "col", axis=1, tiled=True),
    )
    normed_rows, left_rows = rows_blocks(
        pair_rows, valid_rows, valid_all, pair_gain, left_weight, col_count, flat_rows
    )
    pair_tile = lax.dynamic_index_in_dim(
        pair_rows.reshape(block_rows, row_count, col_count, flat_rows, channels),
        col_index,
        2,
        False,
    ).reshape(block_rows, block_cols, channels)
    normed_tile = lax.dynamic_index_in_dim(
        normed_rows.reshape(block_rows, row_count, col_count, flat_rows, channels),
        col_index,
        2,
        False,
    ).reshape(block_rows, block_cols, channels)
    mixed_pairs = jnp.einsum(
        "ikc,jkc->ijc", left_rows, right_cols, preferred_element_type=jnp.float32
    )
    mixed_norm = normalize(mixed_pairs, mix_gain).astype(jnp.bfloat16)
    gate_value = jax.nn.sigmoid(
        jnp.einsum("ijc,ce->ije", normed_tile, gate_weight, preferred_element_type=jnp.float32)
    )
    update = jnp.einsum("ijc,ce->ije", mixed_norm, out_weight, preferred_element_type=jnp.float32)
    pair_new = (pair_tile.astype(jnp.float32) + gate_value * update).astype(jnp.bfloat16)
    bias_input = normalize(pair_new, None).astype(jnp.bfloat16)
    pair_bias = jnp.einsum(
        "ijc,ch->hij", bias_input, bias_weight, preferred_element_type=jnp.float32
    )
    query_heads = query_rows.reshape(samples, block_rows, head_count, head_width)
    key_heads = keys_cols.reshape(samples, block_cols, head_count, head_width)
    value_heads = values_cols.reshape(samples, block_cols, head_count, head_width)
    score_scale = 1.0 / math.sqrt(head_width)
    scores = (
        jnp.einsum("sihd,sjhd->shij", query_heads, key_heads, preferred_element_type=jnp.float32)
        * score_scale
        + pair_bias[None]
    )
    row_ids = row_start + jnp.arange(block_rows, dtype=jnp.int32)
    col_ids = (
        (jnp.arange(row_count, dtype=jnp.int32)[:, None] * col_count + col_index) * flat_rows
        + jnp.arange(flat_rows, dtype=jnp.int32)[None, :]
    ).reshape(block_cols)
    allowed = (valid_cols[None, :] > 0.5) & (chain_rows[:, None] == chain_cols[None, :]) | (
        row_ids[:, None] == col_ids[None, :]
    )
    local_max = jnp.max(jnp.where(allowed[None, None], scores, -1e30), axis=-1)
    row_max = lax.pmax(local_max.astype(jnp.bfloat16), "col").astype(local_max.dtype)
    weights = jnp.where(allowed[None, None], jnp.exp(scores - row_max[..., None]), 0.0).astype(
        jnp.bfloat16
    )
    totals = jnp.sum(weights.astype(jnp.float32), axis=-1)
    summed = jnp.einsum(
        "shij,sjhd->sihd", weights, value_heads, preferred_element_type=jnp.float32
    ).reshape(samples, block_rows, model_width)
    summed_own, totals_own = (
        lax.psum_scatter(
            summed.astype(jnp.bfloat16), "col", scatter_dimension=1, tiled=True
        ).astype(jnp.float32),
        lax.psum_scatter(
            totals.astype(jnp.bfloat16), "col", scatter_dimension=2, tiled=True
        ).astype(jnp.float32),
    )
    attended = (
        summed_own.reshape(samples, flat_rows, head_count, head_width)
        / jnp.transpose(totals_own, (0, 2, 1))[..., None]
    ).astype(jnp.bfloat16)
    attended = attended.reshape(samples, flat_rows, model_width)
    attention_out = jnp.einsum(
        "std,de->ste", attended, merge_weight, preferred_element_type=jnp.float32
    ).astype(jnp.bfloat16)
    return (pair_new.reshape(block_rows, row_count, 1, flat_rows, channels), attention_out)


def solution(mesh):
    in_specs = (
        P(("row", "col"), None, None),
        P(None, ("row", "col"), None),
        P(),
        P(),
        P(),
        P(),
        P(),
        P(),
        P(),
        P(),
        P(),
        P(),
        P(),
    )
    out_specs = (P("row", None, "col", None, None), P(None, ("row", "col"), None))
    return jax.shard_map(shards, mesh=mesh, in_specs=in_specs, out_specs=out_specs, check_vma=False)
```

profile of v0, /device:TPU:0, one launch (start us, length us, event | category | flops | bytes accessed | tf_op | source)
XLA Modules:
  0.0 886.4 jit_solution(9428254966866073664)
XLA Ops:
  21.4 41.2 %all-gather.14.cloned.1.call-done = bf16[16,48,768]{2,0,1:T(8,128)(2,1)} async-done(((bf16[16,6,768]{2,0,1:T(8,128)(2,1)}), bf16[16,48,768]{2,0,1:T(8,128)(2,1)}) %all-gather.14.cloned.1.call-update) | async-done | bytes 1179664 | tf_op jit(solution)/shard_map/all_gather | solution.py:101
  62.6 5.7 reshape.290
  68.4 44.2 %all-gather.10.cloned.1.call-done = bf16[16,48,768]{2,0,1:T(8,128)(2,1)} async-done(((bf16[16,6,768]{2,0,1:T(8,128)(2,1)}), bf16[16,48,768]{2,0,1:T(8,128)(2,1)}) %all-gather.10.cloned.1.call-update) | async-done | bytes 1179664 | tf_op jit(solution)/shard_map/all_gather | solution.py:102
  112.6 4.2 copy.104
  116.8 30.6 %all-gather.12.cloned.1.call-done = bf16[16,96,768]{2,0,1:T(8,128)(2,1)} async-done(((bf16[16,6,768]{2,0,1:T(8,128)(2,1)}), bf16[16,96,768]{2,0,1:T(8,128)(2,1)}) %all-gather.12.cloned.1.call-update) | async-done | bytes 2359312 | tf_op jit(solution)/shard_map/all_gather | solution.py:106
  147.4 4.6 copy.105
  152.0 116.8 %all-gather.8.cloned.1.call-done = bf16[48,768,128]{2,1,0:T(8,128)(2,1)} async-done(((bf16[6,768,128]{2,1,0:T(8,128)(2,1)}), bf16[48,768,128]{2,1,0:T(8,128)(2,1)}) %all-gather.8.cloned.1.call-update) | async-done | bytes 9437200 | tf_op jit(solution)/shard_map/all_gather | solution.py:100
  268.8 13.2 %copy.99 = bf16[48,768,128]{1,0,2:T(8,128)(2,1)} copy(bf16[48,768,128]{2,1,0:T(8,128)(2,1)} %all-gather.8.cloned.1.call-done) | data formatting | bytes 18874368 | tf_op jit(solution)/shard_map/all_gather | solution.py:100
  281.9 87.7 %all-gather.6.cloned.1.call-done = bf16[96,768,128]{2,1,0:T(8,128)(2,1)} async-done(((bf16[6,768,128]{2,1,0:T(8,128)(2,1)}), bf16[96,768,128]{2,1,0:T(8,128)(2,1)}) %all-gather.6.cloned.1.call-update) | async-done | bytes 18874384 | tf_op jit(solution)/shard_map/all_gather | solution.py:105
  369.6 212.1 %while.12 = (s32[]{:T(128)}, bf16[16,6,768,128]{3,2,1,0:T(8,128)(2,1)}, bf16[16,6,768,128]{3,2,1,0:T(8,128)(2,1)}, bf16[16,6,768,128]{3,2,1,0:T(8,128)(2,1)}, f3...) while((s32[]{:T(128)}, ...), condition=%wide.region_3.4_spmd, body=%wide.region_0.0_spmd.sunk | while | flops 314975232 | bytes 16826032 | solution.py:44
  379.1 3.9 fusion.82
  392.4 3.9 fusion.82
  418.9 3.9 fusion.82
  432.1 3.8 fusion.82
  458.6 3.9 fusion.82
  471.9 3.8 fusion.82
  485.1 3.9 fusion.82
  511.6 3.8 fusion.82
  551.4 3.9 fusion.82
  564.7 3.8 fusion.82
  577.9 3.9 fusion.82
  581.7 24.4 %copy.100 = bf16[96,768,128]{1,0,2:T(8,128)(2,1)} copy(bf16[96,768,128]{2,1,0:T(8,128)(2,1)} %bitcast.97) | data formatting | bytes 37748736 | tf_op jit(solution)/shard_map/reshape | solution.py:47
  606.2 12.4 %bitcast_reduce_fusion = (f32[96,48]{0,1:T(8,128)S(1)}, f32[128,48,96]{2,1,0:T(8,128)S(1)}) fusion(bf16[48,768,128]{1,0,2:T(8,128)(2,1)} %copy.99, bf16[96,768,128]{1,0,2:T(8,128)(2,1)} %copy.100), kind=kOutput, calls=%fused_computation.42 | convolution fusion | flops 906554880 | bytes 30689280 | tf_op jit(solution)/shard_map/ikc,jkc->ijc/dot_general | solution.py:123
  624.0 31.1 %reshape_reshape.3 = bf16[96,8,16,6,128]{4,3,2,1,0:T(8,128)(2,1)} reshape(bf16[16,6,768,128]{3,2,1,0:T(8,128)(2,1)} %get-tuple-element.45) | data formatting | bytes 37748736 | tf_op jit(solution)/shard_map/reshape;reshape | solution.py:118
  657.5 16.7 %copy.96 = bf16[96,768,128]{2,0,1:T(8,128)(2,1)S(1)} copy(bf16[96,768,128]{2,1,0:T(8,128)(2,1)} %bitcast.95) | data formatting | bytes 37748736 | tf_op jit(solution)/shard_map/all_gather | solution.py:105
  682.4 9.0 %select_reduce_fusion = (bf16[16,16,96]{2,1,0:T(8,128)(2,1)S(1)}, f32[16,16,96,48]{2,3,1,0:T(8,128)}) fusion(f32[16,96,48]{1,2,0:T(8,128)S(1)} %copy.112, pred[96,48]{0,1:T(8,128)(4,1)S(1)} %compare_or_fusion, bf16[16,96,16,48]{1,3,2,0:T(8,128)(2,1)} %bitcast.101, bf16[16,48,16,48]{3,2,0,1:T(8,128)(2,1)} %reshape.290), kind=kOutput, calls=%fused_computation.34 | convolution fusion | flops 117940224 | bytes 8606208 | tf_op jit(solution)/shard_map/sihd,sjhd->shij/dot_general | solution.py:141
  691.4 55.5 %pmax.7 = bf16[16,16,96]{2,1,0:T(8,128)(2,1)S(1)} all-reduce(bf16[16,16,96]{2,1,0:T(8,128)(2,1)S(1)} %get-tuple-element.90), channel_id=1, replica_groups=mesh['row'=8,'col'=16] {'col'}, use_global_device_ids=true, to_apply=%region_11.12 | all-reduce | flops 24576 | bytes 98304 | tf_op jit(solution)/shard_map/pmax | solution.py:154
  746.9 5.0 fusion.65
  753.3 7.2 convolution_convert_fusion
  760.5 4.9 copy.113
  767.5 44.7 %reduce-scatter.5.cloned.1.call-done = bf16[16,16,6]{1,0,2:T(8,128)(2,1)} async-done(((bf16[16,16,96]{1,0,2:T(8,128)(2,1)}), bf16[16,16,6]{1,0,2:T(8,128)(2,1)}) %reduce-scatter.5.cloned.1.call-update) | async-done | bytes 3088 | tf_op jit(solution)/shard_map/reduce_scatter | solution.py:166
  816.3 60.8 %reduce-scatter.3.cloned.1.call-done = bf16[16,6,768]{2,0,1:T(8,128)(2,1)} async-done(((bf16[16,96,768]{2,0,1:T(8,128)(2,1)}), bf16[16,6,768]{2,0,1:T(8,128)(2,1)}) %reduce-scatter.3.cloned.1.call-update) | async-done | bytes 147472 | tf_op jit(solution)/shard_map/reduce_scatter | solution.py:163
  (228 shorter events, 209.0 us)
Async XLA Ops:
  7.2 2.0 copy-start
  7.2 6.0 copy-start.9
  7.2 55.5 %all-gather.14.cloned.1.call-start = ((), (), s32[]{:S(2)}) async-start(), calls=%async_computation.6 | async-start | bytes 1327104 | tf_op jit(solution)/shard_map/all_gather | solution.py:101
  10.8 4.2 copy-start.2
  10.8 5.7 copy-start.5
  10.8 5.7 copy-start.6
  11.6 100.9 %all-gather.10.cloned.1.call-start = ((), (), s32[]{:S(2)}) async-start(), calls=%async_computation.4 | async-start | bytes 1327104 | tf_op jit(solution)/shard_map/all_gather | solution.py:102
  12.4 135.0 %all-gather.12.cloned.1.call-start = ((), (), s32[]{:S(2)}) async-start(), calls=%async_computation.5 | async-start | bytes 2506752 | tf_op jit(solution)/shard_map/all_gather | solution.py:106
  13.1 255.6 %all-gather.8.cloned.1.call-start = ((), (), s32[]{:S(2)}) async-start(), calls=%async_computation.3 | async-start | bytes 10616832 | tf_op jit(solution)/shard_map/all_gather | solution.py:100
  19.5 1.1 copy-start.8
  19.5 350.1 %all-gather.6.cloned.1.call-start = ((), (), s32[]{:S(2)}) async-start(), calls=%async_computation.2 | async-start | bytes 20054016 | tf_op jit(solution)/shard_map/all_gather | solution.py:105
  20.1 792.1 %reduce-scatter.5.cloned.1.call-start = ((), (), s32[]{:S(2)}) async-start(), calls=%async_computation.8 | async-start | bytes 417792 | tf_op jit(solution)/shard_map/reduce_scatter | solution.py:166
  152.0 217.6 %copy-start.3 = (bf16[128,256]{1,0:T(8,128)(2,1)S(1)}, bf16[128,256]{1,0:T(8,128)(2,1)}, u32[]{:S(2)}) copy-start(bf16[128,256]{1,0:T(8,128)(2,1)} %param.21) | copy-start | bytes 196612
  618.5 0.7 copy-start.10
  674.3 0.8 copy-start.7
  674.7 1.3 copy-start.4
  674.7 1.3 copy-start.11
  676.0 3.6 copy-start.12
  753.0 124.1 %reduce-scatter.3.cloned.1.call-start = ((), (), s32[]{:S(2)}) async-start(), calls=%async_computation.7 | async-start | bytes 2506752 | tf_op jit(solution)/shard_map/reduce_scatter | solution.py:163
  765.7 113.8 %copy-start.1 = (bf16[768,2304]{1,0:T(8,128)(2,1)S(1)}, bf16[768,2304]{1,0:T(8,128)(2,1)}, u32[]{:S(2)}) copy-start(bf16[768,2304]{1,0:T(8,128)(2,1)} %param.26) | copy-start | bytes 10616836
Sparse Core Ops, SparseCore 0:
  11.8 50.8 all-gather.13
  65.5 46.9 all-gather.9
  114.3 33.0 all-gather.11
  150.1 118.6 all-gather.7
  270.3 99.2 all-gather.5
  753.1 59.0 reduce-scatter.4
  814.8 62.2 reduce-scatter.2
where the time goes:
time: 891 us; the launch traced here: 886 us
  waiting for transfers between devices  428 us (48%)
  other arithmetic  170 us (19%)
  local copies, waits for them, and re-layouts  122 us (14%)
  matrix products  95 us (11%)
  blocking collectives  55.5 us (6%)
  between operations  14.5 us (2%)
    all_gather x1, waiting for transfers between devices, shards(): lax.all_gather(right_own, 'row', axis=0, tiled=True)  117 us
    all_gather x1, waiting for transfers between devices, shards(): lax.all_gather(pair_state, 'col', axis=0, tiled=True)  87.7 us
    dynamic_update_slice x32, other arithmetic, rows_blocks(): normed_groups, left_groups = lax.map(one_group, grouped)  87.3 us
    reduce_scatter x1, waiting for transfers between devices, shards(): lax.psum_scatter(summed.astype(jnp.bfloat16), 'col', scatter_dimension=1,...  60.8 us
    dot_general x17, matrix products, gated_branch(): jnp.einsum('ikc,ce->ike', normed, weight, preferred_element_type=jnp.floa...  57.6 us
    pmax x1, blocking collectives, shards(): lax.pmax(local_max.astype(jnp.bfloat16), 'col').astype(local_max.dtype)  55.5 us
    reduce_scatter x1, waiting for transfers between devices, shards(): lax.psum_scatter(totals.astype(jnp.bfloat16), 'col', scatter_dimension=2,...  44.7 us
    all_gather x1, waiting for transfers between devices, shards(): lax.all_gather(values_own, 'row', axis=1, tiled=True)  44.2 us
  transfers between devices with their start and end apart: 7, of which 7 were waited for; matrix products, arithmetic and copies ran while one was open for 6% of the time, Pallas kernels for 0%

commit v1 on v0

--- a/solution.py
+++ b/solution.py
@@ -96,8 +96,11 @@
     normed_own = normalize(pair_state, pair_gain).astype(jnp.bfloat16)
     own_mask = valid_own[:, None] * valid_all[None, :]
     right_own = gated_branch(normed_own, right_weight, own_mask)
+    place_set = lambda s0: jnp.concatenate(
+        lax.all_to_all(jnp.stack([s0 for _ in range(lax.axis_size("row"))]), "row", 0, 0), axis=0
+    )
     right_cols, keys_cols, values_cols = (
-        lax.all_gather(right_own, "row", axis=0, tiled=True),
+        place_set(right_own),
         lax.all_gather(keys_own, "row", axis=1, tiled=True),
         lax.all_gather(values_own, "row", axis=1, tiled=True),
     )

time: 891 us -> 851 us (0.955)
  waiting for transfers between devices: 428 us -> 376 us
    all_gather x1 -> x0, waiting for transfers between devices: 117 us -> none  [shards(): lax.all_gather(right_own, 'row', axis=0, tiled=True)]
    all_gather x1, waiting for transfers between devices: 44.2 us -> 89.4 us  [shards(): lax.all_gather(values_own, 'row', axis=1, tiled=True)]
    all_gather x1, waiting for transfers between devices: 41.2 us -> 63.6 us  [shards(): lax.all_gather(keys_own, 'row', axis=1, tiled=True)]
    all_gather x1 -> x0, local copies, waits for them, and re-layouts: 13.2 us -> none  [shards(): lax.all_gather(right_own, 'row', axis=0, tiled=True)]
    reshape x0 -> x1, local copies, waits for them, and re-layouts: none -> 13.1 us  [shards(): jnp.concatenate(lax.all_to_all(jnp.stack([s0 for _ in range(lax.axis_size...]
  transfers between devices with their start and end apart: 7 -> 7, of which waited for: 7 -> 6; matrix products, arithmetic and copies ran while one was open for 6% -> 7% of each run, Pallas kernels for 0% -> 0%
where the time goes in v1:
time: 851 us; the launch traced here: 846 us
  waiting for transfers between devices  376 us (44%)
  other arithmetic  168 us (20%)
  local copies, waits for them, and re-layouts  128 us (15%)
  matrix products  94.9 us (11%)
  blocking collectives  55.5 us (7%)
  between operations  14.5 us (2%)
    all_gather x1, waiting for transfers between devices, shards(): lax.all_gather(values_own, 'row', axis=1, tiled=True)  89.4 us
    dynamic_update_slice x32, other arithmetic, rows_blocks(): normed_groups, left_groups = lax.map(one_group, grouped)  87.3 us
    all_gather x1, waiting for transfers between devices, shards(): lax.all_gather(pair_state, 'col', axis=0, tiled=True)  85.5 us
    all_gather x1, waiting for transfers between devices, shards(): lax.all_gather(keys_own, 'row', axis=1, tiled=True)  63.6 us
    reduce_scatter x1, waiting for transfers between devices, shards(): lax.psum_scatter(summed.astype(jnp.bfloat16), 'col', scatter_dimension=1,...  60.7 us
    dot_general x17, matrix products, gated_branch(): jnp.einsum('ikc,ce->ike', normed, weight, preferred_element_type=jnp.floa...  57.6 us
    pmax x1, blocking collectives, shards(): lax.pmax(local_max.astype(jnp.bfloat16), 'col').astype(local_max.dtype)  55.5 us
    reduce_scatter x1, waiting for transfers between devices, shards(): lax.psum_scatter(totals.astype(jnp.bfloat16), 'col', scatter_dimension=2,...  44.8 us
  transfers between devices with their start and end apart: 7, of which 6 were waited for; matrix products, arithmetic and copies ran while one was open for 7% of the time, Pallas kernels for 0%

profile of v1, /device:TPU:0, one launch (start us, length us, event | category | flops | bytes accessed | tf_op | source)
XLA Modules:
  0.0 846.3 jit_solution(4060723777575588398)
XLA Ops:
  18.0 5.9 stack.2
  23.9 7.8 all-to-all-start
  33.0 63.6 %all-gather.11.cloned.1.call-done = bf16[16,48,768]{2,0,1:T(8,128)(2,1)} async-done(((bf16[16,6,768]{2,0,1:T(8,128)(2,1)}), bf16[16,48,768]{2,0,1:T(8,128)(2,1)}) %all-gather.11.cloned.1.call-update) | async-done | bytes 1179664 | tf_op jit(solution)/shard_map/all_gather | solution.py:104
  96.6 5.7 reshape.296
  102.3 89.4 %all-gather.7.cloned.1.call-done = bf16[16,48,768]{2,0,1:T(8,128)(2,1)} async-done(((bf16[16,6,768]{2,0,1:T(8,128)(2,1)}), bf16[16,48,768]{2,0,1:T(8,128)(2,1)}) %all-gather.7.cloned.1.call-update) | async-done | bytes 1179664 | tf_op jit(solution)/shard_map/all_gather | solution.py:105
  191.7 4.3 copy.104
  196.0 30.6 %all-gather.9.cloned.1.call-done = bf16[16,96,768]{2,0,1:T(8,128)(2,1)} async-done(((bf16[16,6,768]{2,0,1:T(8,128)(2,1)}), bf16[16,96,768]{2,0,1:T(8,128)(2,1)}) %all-gather.9.cloned.1.call-update) | async-done | bytes 2359312 | tf_op jit(solution)/shard_map/all_gather | solution.py:109
  226.5 4.6 copy.105
  231.1 13.1 %copy.99 = bf16[48,768,128]{1,0,2:T(8,128)(2,1)} copy(bf16[48,768,128]{2,1,0:T(8,128)(2,1)} %bitcast.10) | data formatting | bytes 18874368 | tf_op jit(solution)/shard_map/reshape | solution.py:99
  244.2 85.5 %all-gather.5.cloned.1.call-done = bf16[96,768,128]{2,1,0:T(8,128)(2,1)} async-done(((bf16[6,768,128]{2,1,0:T(8,128)(2,1)}), bf16[96,768,128]{2,1,0:T(8,128)(2,1)}) %all-gather.5.cloned.1.call-update) | async-done | bytes 18874384 | tf_op jit(solution)/shard_map/all_gather | solution.py:108
  329.7 212.1 %while.12 = (s32[]{:T(128)}, bf16[16,6,768,128]{3,2,1,0:T(8,128)(2,1)}, bf16[16,6,768,128]{3,2,1,0:T(8,128)(2,1)}, bf16[16,6,768,128]{3,2,1,0:T(8,128)(2,1)}, f3...) while((s32[]{:T(128)}, ...), condition=%wide.region_3.4_spmd, body=%wide.region_0.0_spmd.sunk | while | flops 314975232 | bytes 16826032 | solution.py:44
  339.2 3.9 fusion.82
  352.4 3.9 fusion.82
  378.9 3.9 fusion.82
  392.2 3.8 fusion.82
  418.7 3.9 fusion.82
  432.0 3.8 fusion.82
  445.2 3.9 fusion.82
  511.5 3.9 fusion.82
  524.7 3.8 fusion.82
  538.0 3.9 fusion.82
  541.8 24.4 %copy.100 = bf16[96,768,128]{1,0,2:T(8,128)(2,1)} copy(bf16[96,768,128]{2,1,0:T(8,128)(2,1)} %bitcast.98) | data formatting | bytes 37748736 | tf_op jit(solution)/shard_map/reshape | solution.py:47
  566.2 12.4 %bitcast_reduce_fusion = (f32[96,48]{0,1:T(8,128)S(1)}, f32[128,48,96]{2,1,0:T(8,128)S(1)}) fusion(bf16[48,768,128]{1,0,2:T(8,128)(2,1)} %copy.99, bf16[96,768,128]{1,0,2:T(8,128)(2,1)} %copy.100), kind=kOutput, calls=%fused_computation.42 | convolution fusion | flops 906554880 | bytes 30689280 | tf_op jit(solution)/shard_map/ikc,jkc->ijc/dot_general | solution.py:126
  584.1 31.1 %reshape_reshape.3 = bf16[96,8,16,6,128]{4,3,2,1,0:T(8,128)(2,1)} reshape(bf16[16,6,768,128]{3,2,1,0:T(8,128)(2,1)} %get-tuple-element.45) | data formatting | bytes 37748736 | tf_op jit(solution)/shard_map/reshape;reshape | solution.py:121
  617.6 16.7 %copy.96 = bf16[96,768,128]{2,0,1:T(8,128)(2,1)S(1)} copy(bf16[96,768,128]{2,1,0:T(8,128)(2,1)} %bitcast.96) | data formatting | bytes 37748736 | tf_op jit(solution)/shard_map/all_gather | solution.py:108
  642.5 9.0 %select_reduce_fusion = (bf16[16,16,96]{2,1,0:T(8,128)(2,1)S(1)}, f32[16,16,96,48]{2,3,1,0:T(8,128)}) fusion(f32[16,96,48]{1,2,0:T(8,128)S(1)} %copy.112, pred[96,48]{0,1:T(8,128)(4,1)S(1)} %compare_or_fusion, bf16[16,96,16,48]{1,3,2,0:T(8,128)(2,1)} %bitcast.102, bf16[16,48,16,48]{3,2,0,1:T(8,128)(2,1)} %reshape.296), kind=kOutput, calls=%fused_computation.34 | convolution fusion | flops 117940224 | bytes 8606208 | tf_op jit(solution)/shard_map/sihd,sjhd->shij/dot_general | solution.py:144
  651.4 55.5 %pmax.7 = bf16[16,16,96]{2,1,0:T(8,128)(2,1)S(1)} all-reduce(bf16[16,16,96]{2,1,0:T(8,128)(2,1)S(1)} %get-tuple-element.90), channel_id=1, replica_groups=mesh['row'=8,'col'=16] {'col'}, use_global_device_ids=true, to_apply=%region_11.12 | all-reduce | flops 24576 | bytes 98304 | tf_op jit(solution)/shard_map/pmax | solution.py:157
  707.0 5.0 fusion.65
  713.3 7.2 convolution_convert_fusion
  720.5 4.9 copy.113
  727.5 44.8 %reduce-scatter.5.cloned.1.call-done = bf16[16,16,6]{1,0,2:T(8,128)(2,1)} async-done(((bf16[16,16,96]{1,0,2:T(8,128)(2,1)}), bf16[16,16,6]{1,0,2:T(8,128)(2,1)}) %reduce-scatter.5.cloned.1.call-update) | async-done | bytes 3088 | tf_op jit(solution)/shard_map/reduce_scatter | solution.py:169
  776.3 60.7 %reduce-scatter.3.cloned.1.call-done = bf16[16,6,768]{2,0,1:T(8,128)(2,1)} async-done(((bf16[16,96,768]{2,0,1:T(8,128)(2,1)}), bf16[16,6,768]{2,0,1:T(8,128)(2,1)}) %reduce-scatter.3.cloned.1.call-update) | async-done | bytes 147472 | tf_op jit(solution)/shard_map/reduce_scatter | solution.py:166
  (228 shorter events, 210.7 us)
Async XLA Ops:
  7.2 2.0 copy-start
  7.2 89.4 %all-gather.11.cloned.1.call-start = ((), (), s32[]{:S(2)}) async-start(), calls=%async_computation.6 | async-start | bytes 1327104 | tf_op jit(solution)/shard_map/all_gather | solution.py:104
  10.8 2.9 copy-start.9
  10.8 3.0 copy-start.2
  10.8 4.9 copy-start.5
  10.8 4.9 copy-start.6
  11.7 180.0 %all-gather.7.cloned.1.call-start = ((), (), s32[]{:S(2)}) async-start(), calls=%async_computation.4 | async-start | bytes 1327104 | tf_op jit(solution)/shard_map/all_gather | solution.py:105
  12.4 214.1 %all-gather.9.cloned.1.call-start = ((), (), s32[]{:S(2)}) async-start(), calls=%async_computation.5 | async-start | bytes 2506752 | tf_op jit(solution)/shard_map/all_gather | solution.py:109
  13.1 316.6 %all-gather.5.cloned.1.call-start = ((), (), s32[]{:S(2)}) async-start(), calls=%async_computation.3 | async-start | bytes 20054016 | tf_op jit(solution)/shard_map/all_gather | solution.py:108
  23.9 8.3 copy-start.8
  23.9 207.3 %all-to-all-start = ((bf16[8,6,768,128]{3,2,1,0:T(8,128)(2,1)}), bf16[8,6,768,128]{3,2,1,0:T(8,128)(2,1)}, u32[]{:S(2)}, u32[]{:S(2)}) async-start(bf16[8,6,768,128]{3,2,1,0:T(8,128)(2,1)} %stack.2), calls=%async_computation | async-start | bytes 18874368 | tf_op jit(solution)/shard_map/all_to_all | solution.py:100
  31.7 740.6 %reduce-scatter.5.cloned.1.call-start = ((), (), s32[]{:S(2)}) async-start(), calls=%async_computation.8 | async-start | bytes 417792 | tf_op jit(solution)/shard_map/reduce_scatter | solution.py:169
  231.1 98.6 %copy-start.3 = (bf16[128,256]{1,0:T(8,128)(2,1)S(1)}, bf16[128,256]{1,0:T(8,128)(2,1)}, u32[]{:S(2)}) copy-start(bf16[128,256]{1,0:T(8,128)(2,1)} %param.21) | copy-start | bytes 196612
  578.6 0.7 copy-start.10
  634.4 0.8 copy-start.7
  634.8 1.3 copy-start.4
  634.8 1.3 copy-start.11
  636.1 3.6 copy-start.12
  713.0 124.0 %reduce-scatter.3.cloned.1.call-start = ((), (), s32[]{:S(2)}) async-start(), calls=%async_computation.7 | async-start | bytes 2506752 | tf_op jit(solution)/shard_map/reduce_scatter | solution.py:166
  725.7 113.7 %copy-start.1 = (bf16[768,2304]{1,0:T(8,128)(2,1)S(1)}, bf16[768,2304]{1,0:T(8,128)(2,1)}, u32[]{:S(2)}) copy-start(bf16[768,2304]{1,0:T(8,128)(2,1)} %param.26) | copy-start | bytes 10616836
Sparse Core Ops, SparseCore 0:
  11.8 84.7 all-gather.10
  99.5 92.1 all-gather.6
  193.4 33.0 all-gather.8
  228.1 101.5 all-gather.4
  713.2 59.0 reduce-scatter.4
  774.7 62.3 reduce-scatter.2
